TPU v7x, 512 devices: a whole 4x4x16 slice. The times are simulated.
512 devices in a mesh: head: 16 (over z), ctx: 32 (over x, y, core).
Axes of the slice: x: 4, y: 4, z: 16, core: 2. Of those that a mesh axis runs over, the one named last changes fastest.
Arguments:
- queries: bfloat16 [2, 8192, 4096], P(None, 'ctx', 'head'), may hold values from -6 to 6
- key_vectors: bfloat16 [2, 8192, 4096], P(None, 'ctx', 'head'), may hold values from -6 to 6
- value_vectors: bfloat16 [2, 8192, 4096], P(None, 'ctx', 'head'), may hold values from -6 to 6
- gate_weight: bfloat16 [16, 256, 512], P('head'), may hold values from -0.375 to 0.375
- up_weight: bfloat16 [16, 256, 512], P('head'), may hold values from -0.375 to 0.375
- down_weight: bfloat16 [16, 256, 512], P('head'), may hold values from -0.25 to 0.25
- learn_rates: float32 [16], P('head'), may hold values from 0.2 to 1
Outputs:
- outputs: bfloat16 [2, 8192, 4096], P(None, ('ctx', 'head'))
All inputs are finite; a program needn't handle non-finite values.
Results may differ from a plain program's by a relative error of at most 0.018.
Values may be sent and summed in bfloat16 or wider, within the bound.
A program may use at most 64 MiB of HBM per device.

v0:
```python
import jax
import jax.numpy as jnp
from jax import lax
from jax.sharding import Mesh
from jax.sharding import PartitionSpec as P

BLOCKS = 2
NS_ITERS = 3
CTX = ("ctx_0", "ctx_1", "ctx_2")
CTX_HEAD = ("ctx_0", "ctx_1", "ctx_2", "head")


COEF_A = 3.4445
COEF_B = -4.775
COEF_C = 2.0315
EPSILON = 1e-06


def in_blocks(shard, dim, devices):
    before, after = (shard.shape[:dim], shard.shape[dim + 1 :])
    return jnp.moveaxis(shard.reshape(*before, devices, -1, *after), dim, 0)


def sum_at_owner(shard, axis, dim):
    devices = lax.axis_size(axis)
    tiles = lax.all_to_all(in_blocks(shard, dim, devices), axis, 0, 0, tiled=True)
    return jnp.sum(tiles, axis=0)


def sent_together(arrays, axis, dim, along):
    widths = [a.shape[along] for a in arrays]
    both = jnp.concatenate(arrays, axis=along)
    result = sum_at_owner(both, axis, dim)
    return tuple(jnp.split(result, [sum(widths[:k]) for k in range(1, len(widths))], axis=along))


def from_everyone(shard, axis):
    copies = jnp.broadcast_to(shard, (lax.axis_size(axis), *shard.shape))
    return lax.all_to_all(copies, axis, split_axis=0, concat_axis=0, tiled=True)


def of_everyone(shard, axis):
    return from_everyone(shard, axis).sum(axis=0)


def together(arrays, axis):
    ends = [0]
    for a in arrays:
        ends.append(ends[-1] + a.size)
    subtotal = of_everyone(jnp.concatenate([a.ravel() for a in arrays]), axis)
    return tuple((subtotal[b:e].reshape(a.shape) for a, b, e in zip(arrays, ends, ends[1:])))


def in_order(tiles, dim):
    tiles = jnp.moveaxis(tiles, 0, dim)
    dims = tiles.shape
    return tiles.reshape(*dims[:dim], dims[dim] * dims[dim + 1], *dims[dim + 2 :])


def whole_of(shard, axes, dim):
    far, near = axes
    tiles = from_everyone(from_everyone(shard, far), near)
    return in_order(tiles.swapaxes(0, 1).reshape(-1, *shard.shape), dim)


def side_by_side(arrays, axis, dim, along):
    both = jnp.concatenate(arrays, axis=along)
    result, at, outs = (whole_of(both, axis, dim), 0, [])
    for a in arrays:
        outs.append(lax.slice_in_dim(result, at, at + a.shape[along], axis=along))
        at += a.shape[along]
    return tuple(outs)


def orthogonalize(iterate):
    for turn_index in range(NS_ITERS):
        gram_matrix = jnp.einsum("gdf,gef->gde", iterate, iterate, precision=lax.Precision.HIGHEST)
        squared = jnp.einsum(
            "gde,gef->gdf", gram_matrix, gram_matrix, precision=lax.Precision.HIGHEST
        )
        polynomial = COEF_B * gram_matrix + COEF_C * squared
        product = jnp.einsum("gde,gef->gdf", polynomial, iterate, precision=lax.Precision.HIGHEST)
        iterate = COEF_A * iterate + product
    return iterate


def scaled(matrix, total_sq):
    return matrix / (jnp.sqrt(total_sq) + EPSILON)[:, None, None]


def reduced(grad_gate, grad_up, grad_down):
    shares = sent_together((grad_gate, grad_up, grad_down), CTX, 1, 0)
    squares = together(
        (
            jnp.sum(shares[0] * shares[0], axis=(1, 2)),
            jnp.sum(shares[1] * shares[1], axis=(1, 2)),
            jnp.sum(shares[2] * shares[2], axis=(1, 2)),
        ),
        CTX,
    )
    first = scaled(shares[0], squares[0])
    second = scaled(shares[1], squares[1])
    third = scaled(shares[2], squares[2])
    normed = side_by_side((first, second, third), (("ctx_0", "ctx_1"), "ctx_2"), 1, 0)
    return tuple((orthogonalize(matrix) for matrix in normed))


def on_device(
    queries, key_vectors, value_vectors, gate_weight, up_weight, down_weight, learn_rates
):
    local_heads = gate_weight.shape[0]
    head_size = gate_weight.shape[1]
    tok_rows = queries.shape[1]
    weights_f = [
        gate_weight.astype(jnp.float32),
        up_weight.astype(jnp.float32),
        down_weight.astype(jnp.float32),
    ]
    weights_b = [gate_weight, up_weight, down_weight]
    results = []
    for block_index in range(BLOCKS):
        keys_h = key_vectors[block_index].reshape(tok_rows, local_heads, head_size)
        values_h = value_vectors[block_index].reshape(tok_rows, local_heads, head_size)
        pre_gate = jnp.einsum(
            "tgd,gdf->gtf", keys_h, weights_b[0], preferred_element_type=jnp.float32
        )
        pre_up = jnp.einsum(
            "tgd,gdf->gtf", keys_h, weights_b[1], preferred_element_type=jnp.float32
        )
        sigmoid_g = jax.nn.sigmoid(pre_gate)
        activated = pre_gate * sigmoid_g
        gated = (activated * pre_up).astype(jnp.bfloat16)
        back = -jnp.einsum(
            "tgd,gdf->gtf", values_h, weights_b[2], preferred_element_type=jnp.float32
        )
        d_up = (back * activated).astype(jnp.bfloat16)
        d_gate = (back * pre_up * sigmoid_g * (1.0 + pre_gate * (1.0 - sigmoid_g))).astype(
            jnp.bfloat16
        )
        grad_gate = jnp.einsum("tgd,gtf->gdf", keys_h, d_gate, preferred_element_type=jnp.float32)
        grad_up = jnp.einsum("tgd,gtf->gdf", keys_h, d_up, preferred_element_type=jnp.float32)
        grad_down = -jnp.einsum("tgd,gtf->gdf", values_h, gated, preferred_element_type=jnp.float32)
        finished = reduced(grad_gate, grad_up, grad_down)
        for which in range(3):
            weights_f[which] = weights_f[which] - learn_rates[:, None, None] * finished[which]
            weights_b[which] = weights_f[which].astype(jnp.bfloat16)
        queries_h = queries[block_index].reshape(tok_rows, local_heads, head_size)
        q_gate = jnp.einsum(
            "tgd,gdf->gtf", queries_h, weights_b[0], preferred_element_type=jnp.float32
        )
        q_up = jnp.einsum(
            "tgd,gdf->gtf", queries_h, weights_b[1], preferred_element_type=jnp.float32
        )
        q_gated = (jax.nn.silu(q_gate) * q_up).astype(jnp.bfloat16)
        block_out = jnp.einsum(
            "gtf,gdf->tgd", q_gated, weights_b[2], preferred_element_type=jnp.float32
        )
        block_out = block_out.reshape(tok_rows, local_heads * head_size).astype(jnp.bfloat16)
        results.append(block_out)
    stacked = jnp.stack(results)
    stacked = lax.all_to_all(stacked, "head", split_axis=1, concat_axis=2, tiled=True)
    return stacked


def solution(mesh):
    torus = Mesh(
        mesh.devices.reshape(mesh.shape["head"], 4, 4, 2), ("head", "ctx_0", "ctx_1", "ctx_2")
    )
    in_specs = (
        P(None, CTX, "head"),
        P(None, CTX, "head"),
        P(None, CTX, "head"),
        P("head", None, None),
        P("head", None, None),
        P("head", None, None),
        P("head"),
    )
    out_specs = P(None, CTX_HEAD, None)
    return jax.shard_map(
        on_device, mesh=torus, in_specs=in_specs, out_specs=out_specs, check_vma=False
    )
```

profile of v0, /device:TPU:32, one launch (start us, length us, event | category | flops | bytes accessed | tf_op | source)
XLA Modules:
  0.0 211.3 jit_solution(16803577042611125080)
XLA Ops:
  0.0 1.3 fusion.82
  1.3 1.2 fusion.80
  3.2 0.6 copy-done
  4.1 0.4 convolution_bitcast_fusion.9
  4.7 29.5 %all_to_all.60 = f32[32,3,8,512]{3,2,1,0:T(8,128)S(1)} all-to-all(f32[32,3,8,512]{3,2,1,0:T(8,128)S(1)} %maximum_bitcast_fusion), channel_id=1, replica_groups=mesh['head'=16,'ctx_0'=4,'ctx_1'=4,'ctx_2'=2] {'ctx_0','ctx_1','ctx_2'}, dimensions={0} | all-to-all | bytes 3145728 | tf_op jit(solution)/shard_map/all_to_all | solution.py:26
  34.3 0.7 multiply_reduce_fusion.5
  35.0 2.0 pad_maximum_fusion.3
  37.0 11.3 %all_to_all.61 = f32[32,1,3]{2,1,0:T(1,128)S(1)} all-to-all(f32[32,1,3]{2,1,0:T(1,128)S(1)} %broadcast_in_dim.12), channel_id=1, replica_groups=mesh['head'=16,'ctx_0'=4,'ctx_1'=4,'ctx_2'=2] {'ctx_0','ctx_1','ctx_2'}, dimensions={0} | all-to-all | bytes 768 | tf_op jit(solution)/shard_map/all_to_all | solution.py:39
  48.3 0.7 fusion.143
  51.0 1.0 broadcast_in_dim.13
  52.0 3.6 %all-to-all-start.2 = ((f32[16,3,8,512]{3,2,1,0:T(8,128)}), f32[16,3,8,512]{3,2,1,0:T(8,128)S(1)}, u32[]{:S(2)}, u32[]{:S(2)}) async-start(f32[16,3,8,512]{3,2,1,0:T(8,128)} %broadcast_in_dim.13), calls=%async_computation.2 | async-start | bytes 1572864 | tf_op jit(solution)/shard_map/all_to_all | solution.py:39
  56.3 14.2 %all-to-all-done.2 = f32[16,3,8,512]{3,2,1,0:T(8,128)S(1)} async-done(((f32[16,3,8,512]{3,2,1,0:T(8,128)}), f32[16,3,8,512]{3,2,1,0:T(8,128)S(1)}, u32[]{:S(2)}, u32[]{:S(2)}) %all-to-all-start.2) | async-done | bytes 786464 | tf_op jit(solution)/shard_map/all_to_all | solution.py:39
  70.7 5.0 %all_to_all.62 = f32[2,16,3,8,512]{4,3,1,2,0:T(8,128)S(1)} all-to-all(f32[2,16,3,8,512]{4,3,1,2,0:T(8,128)S(1)} %broadcast_in_dim.14), channel_id=1, replica_groups=mesh['head'=16,'ctx_0'=4,'ctx_1'=4,'ctx_2'=2] {'ctx_2'}, dimensions={0} | all-to-all | bytes 3145728 | tf_op jit(solution)/shard_map/all_to_all | solution.py:39
  75.9 0.6 fusion.67
  76.5 0.6 fusion.69
  77.1 0.6 fusion.68
  78.1 0.6 convolution_add_fusion.17
  78.8 0.6 fusion.144
  79.8 0.6 convolution_add_fusion.16
  80.4 0.6 fusion.145
  81.8 0.6 convolution_add_fusion.11
  82.5 0.6 fusion.148
  83.5 0.6 convolution_add_fusion.10
  84.2 0.6 fusion.149
  85.2 0.7 fusion.19
  86.6 0.6 convolution_add_fusion.14
  87.2 0.6 fusion.146
  88.2 0.6 convolution_add_fusion.13
  88.9 0.9 fusion.147
  90.1 0.7 fusion.18
  91.1 0.7 fusion.17
  92.8 0.4 convolution_bitcast_fusion.7
  93.4 25.9 %all_to_all.63 = f32[32,3,8,512]{3,2,1,0:T(8,128)S(1)} all-to-all(f32[32,3,8,512]{3,2,1,0:T(8,128)S(1)} %maximum_bitcast_fusion.1), channel_id=1, replica_groups=mesh['head'=16,'ctx_0'=4,'ctx_1'=4,'ctx_2'=2] {'ctx_0','ctx_1','ctx_2'}, dimensions={0} | all-to-all | bytes 3145728 | tf_op jit(solution)/shard_map/all_to_all | solution.py:26
  119.4 0.7 multiply_reduce_fusion.2
  120.1 2.0 pad_maximum_fusion.4
  122.1 11.3 %all_to_all.64 = f32[32,1,3]{2,1,0:T(1,128)S(1)} all-to-all(f32[32,1,3]{2,1,0:T(1,128)S(1)} %broadcast_in_dim.15), channel_id=1, replica_groups=mesh['head'=16,'ctx_0'=4,'ctx_1'=4,'ctx_2'=2] {'ctx_0','ctx_1','ctx_2'}, dimensions={0} | all-to-all | bytes 768 | tf_op jit(solution)/shard_map/all_to_all | solution.py:39
  133.4 0.7 fusion.142
  136.1 1.0 broadcast_in_dim.16
  137.1 3.6 %all-to-all-start.6 = ((f32[16,3,8,512]{3,2,1,0:T(8,128)}), f32[16,3,8,512]{3,2,1,0:T(8,128)S(1)}, u32[]{:S(2)}, u32[]{:S(2)}) async-start(f32[16,3,8,512]{3,2,1,0:T(8,128)} %broadcast_in_dim.16), calls=%async_computation.6 | async-start | bytes 1572864 | tf_op jit(solution)/shard_map/all_to_all | solution.py:39
  141.0 1.1 fusion.53
  142.1 13.5 %all-to-all-done.6 = f32[16,3,8,512]{3,2,1,0:T(8,128)S(1)} async-done(((f32[16,3,8,512]{3,2,1,0:T(8,128)}), f32[16,3,8,512]{3,2,1,0:T(8,128)S(1)}, u32[]{:S(2)}, u32[]{:S(2)}) %all-to-all-start.6) | async-done | bytes 786464 | tf_op jit(solution)/shard_map/all_to_all | solution.py:39
  155.8 5.0 %all_to_all.65 = f32[2,16,3,8,512]{4,3,1,2,0:T(8,128)S(1)} all-to-all(f32[2,16,3,8,512]{4,3,1,2,0:T(8,128)S(1)} %broadcast_in_dim.17), channel_id=1, replica_groups=mesh['head'=16,'ctx_0'=4,'ctx_1'=4,'ctx_2'=2] {'ctx_2'}, dimensions={0} | all-to-all | bytes 3145728 | tf_op jit(solution)/shard_map/all_to_all | solution.py:39
  161.0 0.6 fusion.70
  161.6 0.6 fusion.72
  162.2 0.6 fusion.71
  163.2 0.6 convolution_add_fusion.8
  163.9 0.6 fusion.150
  164.9 0.6 convolution_add_fusion.7
  165.5 0.6 fusion.151
  166.9 0.6 convolution_add_fusion.2
  167.5 0.6 fusion.154
  168.5 0.6 convolution_add_fusion.1
  169.2 0.6 fusion.155
  170.6 0.6 convolution_add_fusion.5
  171.2 0.6 fusion.152
  172.2 0.6 convolution_add_fusion.4
  172.9 0.6 fusion.153
  173.9 0.6 fusion.29
  174.8 0.6 fusion.28
  175.4 0.6 fusion.30
  176.1 0.4 fusion.54
  176.5 0.5 copy-done.7
  177.2 33.4 %all_to_all.66 = bf16[2,256,256]{2,0,1:T(2,128)(2,1)S(1)} all-to-all(bf16[2,256,256]{2,0,1:T(2,128)(2,1)S(1)} %copy.128), channel_id=1, replica_groups=mesh['head'=16,'ctx_0'=4,'ctx_1'=4,'ctx_2'=2] {'head'}, dimensions={1} | all-to-all | bytes 524288 | tf_op jit(solution)/shard_map/all_to_all | solution.py:161
  210.6 0.7 copy.146
  (63 shorter events, 11.4 us)
Async XLA Ops:
  0.0 2.5 %copy-start.4 = (bf16[2,256,256]{2,1,0:T(8,128)(2,1)S(1)}, bf16[2,256,256]{2,1,0:T(8,128)(2,1)}, u32[]{:S(2)}) copy-start(bf16[2,256,256]{2,1,0:T(8,128)(2,1)} %param.9) | copy-start | bytes 786436
  0.0 2.6 %copy-start.3 = (bf16[1,256,512]{2,1,0:T(8,128)(2,1)S(1)}, bf16[1,256,512]{2,1,0:T(8,128)(2,1)}, u32[]{:S(2)}) copy-start(bf16[1,256,512]{2,1,0:T(8,128)(2,1)} %param.12) | copy-start | bytes 786436
  2.8 1.0 copy-start
  52.0 18.4 %all-to-all-start.2 = ((f32[16,3,8,512]{3,2,1,0:T(8,128)}), f32[16,3,8,512]{3,2,1,0:T(8,128)S(1)}, u32[]{:S(2)}, u32[]{:S(2)}) async-start(f32[16,3,8,512]{3,2,1,0:T(8,128)} %broadcast_in_dim.13), calls=%async_computation.2 | async-start | bytes 1572864 | tf_op jit(solution)/shard_map/all_to_all | solution.py:39
  83.5 1.7 copy-start.1
  88.2 1.9 copy-start.2
  90.9 1.0 copy-start.5
  119.4 21.3 %copy-start.6 = (bf16[2,256,256]{2,1,0:T(8,128)(2,1)S(1)}, bf16[2,256,256]{2,1,0:T(8,128)(2,1)}, u32[]{:S(2)}) copy-start(bf16[2,256,256]{2,1,0:T(8,128)(2,1)} %param.7) | copy-start | bytes 786436
  137.1 18.4 %all-to-all-start.6 = ((f32[16,3,8,512]{3,2,1,0:T(8,128)}), f32[16,3,8,512]{3,2,1,0:T(8,128)S(1)}, u32[]{:S(2)}, u32[]{:S(2)}) async-start(f32[16,3,8,512]{3,2,1,0:T(8,128)} %broadcast_in_dim.16), calls=%async_computation.6 | async-start | bytes 1572864 | tf_op jit(solution)/shard_map/all_to_all | solution.py:39
  176.1 0.9 copy-start.7
where the time goes:
time: 212 us; the launch traced here: 211 us
  blocking collectives  121 us (57%)
  matrix products  37.7 us (18%)
  waiting for transfers between devices  27.6 us (13%)
  starting transfers between devices  7.23 us (3%)
  local copies, waits for them, and re-layouts  6.14 us (3%)
  other arithmetic  5.97 us (3%)
  between operations  5.44 us (3%)
    all_to_all x2, blocking collectives, sum_at_owner(): lax.all_to_all(in_blocks(shard, dim, devices), axis, 0, 0, tiled=True)  55.3 us
    all_to_all x1, blocking collectives, on_device(): lax.all_to_all(stacked, 'head', split_axis=1, concat_axis=2, tiled=True)  33.4 us
    all_to_all x4, blocking collectives, from_everyone(): return lax.all_to_all(copies, axis, split_axis=0, concat_axis=0, tiled=True)  32.6 us
    all_to_all x2, waiting for transfers between devices, from_everyone(): return lax.all_to_all(copies, axis, split_axis=0, concat_axis=0, tiled=True)  27.6 us
    dot_general x18, matrix products, orthogonalize(): jnp.einsum('gde,gef->gdf', polynomial, iterate, precision=lax.Precision.H...  11.8 us
    dot_general x18, matrix products, orthogonalize(): jnp.einsum('gdf,gef->gde', iterate, iterate, precision=lax.Precision.HIGH...  11.3 us
    all_to_all x2, starting transfers between devices, from_everyone(): return lax.all_to_all(copies, axis, split_axis=0, concat_axis=0, tiled=True)  7.23 us
    dot_general x18, matrix products, orthogonalize(): jnp.einsum('gde,gef->gdf', gram_matrix, gram_matrix, precision=lax.Precis...  6.87 us
  transfers between devices with their start and end apart: 2, of which 2 were waited for; matrix products, arithmetic and copies ran while one was open for 1% of the time, Pallas kernels for 0%

commit v1 on v0

v1 whole, which is shorter than its diff:
```python
import jax
import jax.numpy as jnp
from jax import lax
from jax.experimental import pallas as pl
from jax.experimental.pallas import tpu as pltpu
from jax.sharding import PartitionSpec as P

BLOCKS = 2
NS_ITERS = 3
COEF_A = 3.4445
COEF_B = -4.775
COEF_C = 2.0315
EPSILON = 1e-06

SIDE = 4
CHIPS = SIDE * SIDE
HEADS = 16
DH = 256
FH = 512
HALF = 256
OWN = DH // CHIPS
MESH = pl.DeviceIdType.MESH

STEPS = sorted(
    [(dx, dy) for dx in range(SIDE) for dy in range(SIDE) if (dx, dy) != (0, 0)],
    key=lambda s: -(min(s[0], SIDE - s[0]) + min(s[1], SIDE - s[1])),
)
HOPS = sorted(range(1, HEADS), key=lambda o: -min(o, HEADS - o))


def nn(a, b):
    return jnp.dot(a, b, preferred_element_type=jnp.float32)


def nt(a, b):
    return lax.dot_general(a, b, (((1,), (1,)), ((), ())), preferred_element_type=jnp.float32)


def kernel(
    lr_ref,
    q_ref,
    k_ref,
    v_ref,
    wg_ref,
    wu_ref,
    wd_ref,
    out_ref,
    mine,
    theirs,
    pairs,
    shares,
    whole,
    master,
    fast,
    iterate,
    made,
    pair_s,
    pair_r,
    share_s,
    share_r,
    whole_s,
    whole_r,
    twin_s,
    twin_r,
    out_s,
    out_r,
):
    bf16, f32 = jnp.bfloat16, jnp.float32
    head = lax.axis_index("head")
    ctx = lax.axis_index("ctx")
    core = ctx % 2
    chip = ctx // 2
    x, y = chip // SIDE, chip % SIDE
    twin = {"ctx": ctx + 1 - 2 * core}

    def to_chip(step, sign=1):
        return (x + sign * step[0] + SIDE) % SIDE * SIDE + (y + sign * step[1] + SIDE) % SIDE

    def on_chip(other):
        return {"ctx": other * 2 + core}

    def send(src, dst, s, r, device):
        return pltpu.make_async_remote_copy(
            src_ref=src,
            dst_ref=dst,
            send_sem=s,
            recv_sem=r,
            device_id=device,
            device_id_type=MESH,
        )

    barrier = pltpu.get_barrier_semaphore()
    for o in HOPS:
        pl.semaphore_signal(
            barrier, inc=1, device_id={"head": (head + o) % HEADS}, device_id_type=MESH
        )
    for step in STEPS:
        pl.semaphore_signal(
            barrier, inc=1, device_id=on_chip(to_chip(step)), device_id_type=MESH
        )
    pl.semaphore_signal(barrier, inc=1, device_id=twin, device_id_type=MESH)

    master[0] = wg_ref[0].astype(f32)
    master[1] = wu_ref[0].astype(f32)
    master[2] = wd_ref[0].astype(f32)
    fast[0] = wg_ref[0]
    fast[1] = wu_ref[0]
    fast[2] = wd_ref[0]

    def pair_copy(b, m):
        return send(
            mine.at[b, 1 - core, m], theirs.at[b, m], pair_s.at[b, m], pair_r.at[b, m], twin
        )

    def share_copy(b, i):
        other = to_chip(STEPS[i])
        return send(
            pairs.at[b, other], shares.at[b, i], share_s.at[b, i], share_r.at[b, i], on_chip(other)
        )

    def whole_copy(b, i):
        here = whole.at[b, core, chip]
        return send(
            here, here, whole_s.at[b, i], whole_r.at[b, i], on_chip(to_chip(STEPS[i]))
        )

    def twin_copy(b, i):
        slot = chip if i == len(STEPS) else to_chip(STEPS[i], -1)
        here = whole.at[b, core, slot]
        return send(here, here, twin_s.at[b, i], twin_r.at[b, i], twin)

    def out_copy(b, i):
        other = (head + HOPS[i]) % HEADS
        columns = pl.ds(pl.multiple_of(head * DH, DH), DH)
        return send(
            made.at[b, other],
            out_ref.at[b, :, columns],
            out_s.at[b, i],
            out_r.at[b, i],
            {"head": other},
        )

    def gradients(b):
        keys, values = k_ref[b], v_ref[b]
        gate = nn(keys, fast[0])
        up = nn(keys, fast[1])
        sig = jax.nn.sigmoid(gate)
        act = gate * sig
        gated = (act * up).astype(bf16)
        values_t = values.T
        for j in range(2):
            mine[b, j, 2] = nn(values_t, gated[:, j * HALF : (j + 1) * HALF]).astype(bf16)
        back = nn(values, fast[2])
        d_up = (back * act).astype(bf16)
        d_gate = (back * up * sig * (1.0 + gate * (1.0 - sig))).astype(bf16)
        keys_t = keys.T
        for m, d in ((0, d_gate), (1, d_up)):
            for j in range(2):
                mine[b, j, m] = nn(keys_t, d[:, j * HALF : (j + 1) * HALF]).astype(bf16)

    def start_pair(b):
        for m in (2, 0, 1):
            pair_copy(b, m).start()

    def start_shares(b):
        for m in (2, 0, 1):
            pair_copy(b, m).wait_recv()
            both = mine[b, core, m].astype(f32) + theirs[b, m].astype(f32)
            pairs[b, :, m] = both.astype(bf16).reshape(CHIPS, OWN, HALF)
        for i in range(len(STEPS)):
            share_copy(b, i).start()

    def finish_shares(b):
        total = pairs[b, chip].astype(f32)
        for i in range(len(STEPS)):
            share_copy(b, i).wait_recv()
            total = total + shares[b, i].astype(f32)
        whole[b, core, chip] = total.astype(bf16)
        for i in range(len(STEPS)):
            whole_copy(b, i).start()
        twin_copy(b, len(STEPS)).start()
        for i in range(len(STEPS)):
            whole_copy(b, i).wait_recv()
            twin_copy(b, i).start()
        for i in range(len(STEPS) + 1):
            twin_copy(b, i).wait_recv()

    def update(b):
        for m in range(3):
            grad = jnp.concatenate(
                [whole[b, j, :, m].reshape(DH, HALF) for j in range(2)], axis=1
            )
            grad_f = grad.astype(f32)
            inv = 1.0 / (jnp.sqrt(jnp.sum(grad_f * grad_f, keepdims=True)) + EPSILON)
            gram = nt(grad, grad) * inv * inv
            gram_b = gram.astype(bf16)
            poly = COEF_B * gram + COEF_C * nn(gram_b, gram_b)
            iterate[m] = (COEF_A * grad_f + nn(poly.astype(bf16), grad)) * inv
        for turn in range(1, NS_ITERS):
            for m in range(3):
                now = iterate[m]
                now_b = now.astype(bf16)
                gram = nt(now_b, now_b)
                gram_b = gram.astype(bf16)
                poly = COEF_B * gram + COEF_C * nn(gram_b, gram_b)
                iterate[m] = COEF_A * now + nn(poly.astype(bf16), now_b)
        for m in range(3):
            moved = master[m] + lr_ref[0] * iterate[m]
            master[m] = moved
            fast[m] = moved.astype(bf16)

    def answer(b):
        rows = q_ref[b]
        gate = nn(rows, fast[0])
        up = nn(rows, fast[1])
        gated = (gate * jax.nn.sigmoid(gate) * up).astype(bf16)
        made[b] = nt(gated, fast[2]).astype(bf16).reshape(HEADS, OWN, DH)
        for i in range(len(HOPS)):
            out_copy(b, i).start()
        columns = pl.ds(pl.multiple_of(head * DH, DH), DH)
        out_ref[b, :, columns] = made[b, head]

    gradients(0)
    pl.semaphore_wait(barrier, len(HOPS) + len(STEPS) + 1)
    start_pair(0)
    start_shares(0)
    finish_shares(0)
    update(0)
    gradients(1)
    start_pair(1)
    start_shares(1)
    answer(0)
    finish_shares(1)
    update(1)
    answer(1)
    for b in range(BLOCKS):
        for m in range(3):
            pair_copy(b, m).wait_send()
        for i in range(len(STEPS)):
            share_copy(b, i).wait_send()
            whole_copy(b, i).wait_send()
        for i in range(len(STEPS) + 1):
            twin_copy(b, i).wait_send()
        for i in range(len(HOPS)):
            out_copy(b, i).wait()


def on_device(queries, key_vectors, value_vectors, gate_weight, up_weight, down_weight, learn_rates):
    bf16, f32 = jnp.bfloat16, jnp.float32
    others, hops = len(STEPS), len(HOPS)
    vmem = pl.BlockSpec(memory_space=pltpu.VMEM)
    dma = pltpu.SemaphoreType.DMA
    return pl.pallas_call(
        kernel,
        out_shape=jax.ShapeDtypeStruct((BLOCKS, OWN, HEADS * DH), bf16),
        in_specs=[pl.BlockSpec(memory_space=pltpu.SMEM)] + [vmem] * 6,
        out_specs=vmem,
        scratch_shapes=[
            pltpu.VMEM((BLOCKS, 2, 3, DH, HALF), bf16),
            pltpu.VMEM((BLOCKS, 3, DH, HALF), bf16),
            pltpu.VMEM((BLOCKS, CHIPS, 3, OWN, HALF), bf16),
            pltpu.VMEM((BLOCKS, others, 3, OWN, HALF), bf16),
            pltpu.VMEM((BLOCKS, 2, CHIPS, 3, OWN, HALF), bf16),
            pltpu.VMEM((3, DH, FH), f32),
            pltpu.VMEM((3, DH, FH), bf16),
            pltpu.VMEM((3, DH, FH), f32),
            pltpu.VMEM((BLOCKS, HEADS, OWN, DH), bf16),
            dma((BLOCKS, 3)),
            dma((BLOCKS, 3)),
            dma((BLOCKS, others)),
            dma((BLOCKS, others)),
            dma((BLOCKS, others)),
            dma((BLOCKS, others)),
            dma((BLOCKS, others + 1)),
            dma((BLOCKS, others + 1)),
            dma((BLOCKS, hops)),
            dma((BLOCKS, hops)),
        ],
        compiler_params=pltpu.CompilerParams(
            collective_id=0, has_side_effects=True, vmem_limit_bytes=48 * 1024 * 1024
        ),
        name="ttt",
    )(learn_rates, queries, key_vectors, value_vectors, gate_weight, up_weight, down_weight)


def solution(mesh):
    return jax.shard_map(
        on_device,
        mesh=mesh,
        in_specs=(
            P(None, "ctx", "head"),
            P(None, "ctx", "head"),
            P(None, "ctx", "head"),
            P("head", None, None),
            P("head", None, None),
            P("head", None, None),
            P("head"),
        ),
        out_specs=P(None, ("ctx", "head"), None),
        check_vma=False,
    )
```

time: 212 us -> 76.9 us (0.36)
  the two profiles are of different devices: /device:TPU:32 before, /device:TPU:1 now
where the time goes in v1:
time: 76.9 us; the launch traced here: 76.6 us
  Pallas kernels  69.6 us (91%)
  local copies, waits for them, and re-layouts  6.4 us (8%)
    pallas_call x1, Pallas kernels, on_device(): pl.pallas_call(kernel, out_shape=jax.ShapeDtypeStruct((BLOCKS, OWN, HEADS...  69.6 us
    unnamed x13, local copies, waits for them, and re-layouts  6.4 us

profile of v1, /device:TPU:1, one launch (start us, length us, event | category | flops | bytes accessed | tf_op | source)
XLA Modules:
  0.0 76.6 jit_solution(18193947242912112693)
XLA Ops:
  0.7 0.0 copy-start
  0.7 0.9 %copy-done = bf16[2,256,256]{2,1,0:T(8,128)(2,1)S(1)} copy-done((bf16[2,256,256]{2,1,0:T(8,128)(2,1)S(1)}, bf16[2,256,256]{2,1,0:T(8,128)(2,1)}, u32[]{:S(2)}) %copy-start) | copy-done | bytes 262168
  1.6 0.0 copy-start.1
  1.6 0.9 %copy-done.1 = bf16[2,256,256]{2,1,0:T(8,128)(2,1)S(1)} copy-done((bf16[2,256,256]{2,1,0:T(8,128)(2,1)S(1)}, bf16[2,256,256]{2,1,0:T(8,128)(2,1)}, u32[]{:S(2)}) %copy-start.1) | copy-done | bytes 262168
  2.6 0.0 copy-start.2
  2.6 0.9 %copy-done.2 = bf16[2,256,256]{2,1,0:T(8,128)(2,1)S(1)} copy-done((bf16[2,256,256]{2,1,0:T(8,128)(2,1)S(1)}, bf16[2,256,256]{2,1,0:T(8,128)(2,1)}, u32[]{:S(2)}) %copy-start.2) | copy-done | bytes 262168
  3.5 0.0 copy-start.3
  3.5 0.9 %copy-done.3 = bf16[1,256,512]{2,1,0:T(8,128)(2,1)S(1)} copy-done((bf16[1,256,512]{2,1,0:T(8,128)(2,1)S(1)}, bf16[1,256,512]{2,1,0:T(8,128)(2,1)}, u32[]{:S(2)}) %copy-start.3) | copy-done | bytes 262168
  4.5 0.0 copy-start.4
  4.5 0.9 %copy-done.4 = bf16[1,256,512]{2,1,0:T(8,128)(2,1)S(1)} copy-done((bf16[1,256,512]{2,1,0:T(8,128)(2,1)S(1)}, bf16[1,256,512]{2,1,0:T(8,128)(2,1)}, u32[]{:S(2)}) %copy-start.4) | copy-done | bytes 262168
  5.4 0.0 copy-start.5
  5.4 0.9 %copy-done.5 = bf16[1,256,512]{2,1,0:T(8,128)(2,1)S(1)} copy-done((bf16[1,256,512]{2,1,0:T(8,128)(2,1)S(1)}, bf16[1,256,512]{2,1,0:T(8,128)(2,1)}, u32[]{:S(2)}) %copy-start.5) | copy-done | bytes 262168
  6.4 69.6 %ttt.1 = bf16[2,16,4096]{2,1,0:T(8,128)(2,1)S(1)} custom-call(f32[1]{0:T(128)S(6)} %copy.9.lr_ref, bf16[2,256,256]{2,1,0:T(8,128)(2,1)S(1)} %copy-done, bf16[2,256,256]{2,1,0:T(8,128)(2,1)S(1)} %copy-done.1, bf16[2,256,256]{2,1,0:T(8,128)(2,1)S(1)} %copy-done.2, bf16[1,256,512]{2,1,0:T(8,128)(2,1)S(1)} %copy-done.3, bf16[1,256,512]{2,1,0:T(8,128)(2,1)S(1)} %copy-done.4, ...), custom_call_target="tpu_custom_call" | custom-call | tf_op jit(solution)/shard_map/ttt/pallas_call | solution.py:253
  75.9 0.7 copy.10
Async XLA Ops:
  0.7 1.0 %copy-start = (bf16[2,256,256]{2,1,0:T(8,128)(2,1)S(1)}, bf16[2,256,256]{2,1,0:T(8,128)(2,1)}, u32[]{:S(2)}) copy-start(bf16[2,256,256]{2,1,0:T(8,128)(2,1)} %q_ref.1) | copy-start | bytes 786436
  1.6 0.9 %copy-start.1 = (bf16[2,256,256]{2,1,0:T(8,128)(2,1)S(1)}, bf16[2,256,256]{2,1,0:T(8,128)(2,1)}, u32[]{:S(2)}) copy-start(bf16[2,256,256]{2,1,0:T(8,128)(2,1)} %k_ref.1) | copy-start | bytes 786436
  2.6 0.9 %copy-start.2 = (bf16[2,256,256]{2,1,0:T(8,128)(2,1)S(1)}, bf16[2,256,256]{2,1,0:T(8,128)(2,1)}, u32[]{:S(2)}) copy-start(bf16[2,256,256]{2,1,0:T(8,128)(2,1)} %v_ref.1) | copy-start | bytes 786436
  3.5 0.9 %copy-start.3 = (bf16[1,256,512]{2,1,0:T(8,128)(2,1)S(1)}, bf16[1,256,512]{2,1,0:T(8,128)(2,1)}, u32[]{:S(2)}) copy-start(bf16[1,256,512]{2,1,0:T(8,128)(2,1)} %wg_ref.1) | copy-start | bytes 786436
  4.5 0.9 %copy-start.4 = (bf16[1,256,512]{2,1,0:T(8,128)(2,1)S(1)}, bf16[1,256,512]{2,1,0:T(8,128)(2,1)}, u32[]{:S(2)}) copy-start(bf16[1,256,512]{2,1,0:T(8,128)(2,1)} %wu_ref.1) | copy-start | bytes 786436
  5.4 0.9 %copy-start.5 = (bf16[1,256,512]{2,1,0:T(8,128)(2,1)S(1)}, bf16[1,256,512]{2,1,0:T(8,128)(2,1)}, u32[]{:S(2)}) copy-start(bf16[1,256,512]{2,1,0:T(8,128)(2,1)} %wd_ref.1) | copy-start | bytes 786436

commit v2 on v1

--- a/solution.py
+++ b/solution.py
@@ -25,6 +25,7 @@
     [(dx, dy) for dx in range(SIDE) for dy in range(SIDE) if (dx, dy) != (0, 0)],
     key=lambda s: -(min(s[0], SIDE - s[0]) + min(s[1], SIDE - s[1])),
 )
+RING = (1, 2, 4)
 HOPS = sorted(range(1, HEADS), key=lambda o: -min(o, HEADS - o))
 
 
@@ -38,13 +39,16 @@
 
 def kernel(
     lr_ref,
+    q_hbm,
+    k_hbm,
+    v_hbm,
+    wg_hbm,
+    wu_hbm,
+    wd_hbm,
+    out_ref,
     q_ref,
     k_ref,
     v_ref,
-    wg_ref,
-    wu_ref,
-    wd_ref,
-    out_ref,
     mine,
     theirs,
     pairs,
@@ -52,8 +56,8 @@
     whole,
     master,
     fast,
-    iterate,
     made,
+    load_s,
     pair_s,
     pair_r,
     share_s,
@@ -64,6 +68,7 @@
     twin_r,
     out_s,
     out_r,
+    ring,
 ):
     bf16, f32 = jnp.bfloat16, jnp.float32
     head = lax.axis_index("head")
@@ -90,9 +95,9 @@
         )
 
     barrier = pltpu.get_barrier_semaphore()
-    for o in HOPS:
+    for z in (1, HEADS - 1):
         pl.semaphore_signal(
-            barrier, inc=1, device_id={"head": (head + o) % HEADS}, device_id_type=MESH
+            barrier, inc=1, device_id={"head": (head + z) % HEADS}, device_id_type=MESH
         )
     for step in STEPS:
         pl.semaphore_signal(
@@ -100,12 +105,30 @@
         )
     pl.semaphore_signal(barrier, inc=1, device_id=twin, device_id_type=MESH)
 
-    master[0] = wg_ref[0].astype(f32)
-    master[1] = wu_ref[0].astype(f32)
-    master[2] = wd_ref[0].astype(f32)
-    fast[0] = wg_ref[0]
-    fast[1] = wu_ref[0]
-    fast[2] = wd_ref[0]
+    loads = [
+        pltpu.make_async_copy(src, dst, load_s.at[i])
+        for i, (src, dst) in enumerate(
+            (
+                (k_hbm, k_ref),
+                (wg_hbm.at[0], fast.at[0]),
+                (wu_hbm.at[0], fast.at[1]),
+                (v_hbm, v_ref),
+                (wd_hbm.at[0], fast.at[2]),
+                (q_hbm, q_ref),
+            )
+        )
+    ]
+    for load in loads:
+        load.start()
+
+    def ring_signal(level):
+        for z in (RING[level], HEADS - RING[level]):
+            pl.semaphore_signal(
+                ring.at[level], inc=1, device_id={"head": (head + z) % HEADS}, device_id_type=MESH
+            )
+
+    def ring_wait(level):
+        pl.semaphore_wait(ring.at[level], 2)
 
     def pair_copy(b, m):
         return send(
@@ -141,12 +164,19 @@
         )
 
     def gradients(b):
-        keys, values = k_ref[b], v_ref[b]
+        if b == 0:
+            for load in loads[:3]:
+                load.wait()
+        keys = k_ref[b]
         gate = nn(keys, fast[0])
         up = nn(keys, fast[1])
         sig = jax.nn.sigmoid(gate)
         act = gate * sig
         gated = (act * up).astype(bf16)
+        if b == 0:
+            for load in loads[3:5]:
+                load.wait()
+        values = v_ref[b]
         values_t = values.T
         for j in range(2):
             mine[b, j, 2] = nn(values_t, gated[:, j * HALF : (j + 1) * HALF]).astype(bf16)
@@ -170,7 +200,7 @@
         for i in range(len(STEPS)):
             share_copy(b, i).start()
 
-    def finish_shares(b):
+    def start_wholes(b):
         total = pairs[b, chip].astype(f32)
         for i in range(len(STEPS)):
             share_copy(b, i).wait_recv()
@@ -179,6 +209,8 @@
         for i in range(len(STEPS)):
             whole_copy(b, i).start()
         twin_copy(b, len(STEPS)).start()
+
+    def finish_wholes(b):
         for i in range(len(STEPS)):
             whole_copy(b, i).wait_recv()
             twin_copy(b, i).start()
@@ -186,30 +218,36 @@
             twin_copy(b, i).wait_recv()
 
     def update(b):
+        grads = [
+            jnp.concatenate([whole[b, j, :, m].reshape(DH, HALF) for j in range(2)], axis=1)
+            for m in range(3)
+        ]
+        now = [g.astype(f32) for g in grads]
+        sizes = [jnp.sum(g * g, keepdims=True) for g in now]
+        scales = [1.0 / (jnp.sqrt(size) + EPSILON) for size in sizes]
+        now_b = grads
+        for turn in range(NS_ITERS):
+            grams = [nt(g, g) for g in now_b]
+            if turn == 0:
+                grams = [g * s * s for g, s in zip(grams, scales)]
+            grams_b = [g.astype(bf16) for g in grams]
+            polys = [COEF_B * g + COEF_C * nn(h, h) for g, h in zip(grams, grams_b)]
+            now = [
+                COEF_A * g + nn(poly.astype(bf16), h) for g, poly, h in zip(now, polys, now_b)
+            ]
+            if turn == 0:
+                now = [g * s for g, s in zip(now, scales)]
+            now_b = [g.astype(bf16) for g in now]
         for m in range(3):
-            grad = jnp.concatenate(
-                [whole[b, j, :, m].reshape(DH, HALF) for j in range(2)], axis=1
-            )
-            grad_f = grad.astype(f32)
-            inv = 1.0 / (jnp.sqrt(jnp.sum(grad_f * grad_f, keepdims=True)) + EPSILON)
-            gram = nt(grad, grad) * inv * inv
-            gram_b = gram.astype(bf16)
-            poly = COEF_B * gram + COEF_C * nn(gram_b, gram_b)
-            iterate[m] = (COEF_A * grad_f + nn(poly.astype(bf16), grad)) * inv
-        for turn in range(1, NS_ITERS):
-            for m in range(3):
-                now = iterate[m]
-                now_b = now.astype(bf16)
-                gram = nt(now_b, now_b)
-                gram_b = gram.astype(bf16)
-                poly = COEF_B * gram + COEF_C * nn(gram_b, gram_b)
-                iterate[m] = COEF_A * now + nn(poly.astype(bf16), now_b)
-        for m in range(3):
-            moved = master[m] + lr_ref[0] * iterate[m]
-            master[m] = moved
+            before = fast[m].astype(f32) if b == 0 else master[m]
+            moved = before + lr_ref[0] * now[m]
+            if b + 1 < BLOCKS:
+                master[m] = moved
             fast[m] = moved.astype(bf16)
 
     def answer(b):
+        if b == 0:
+            loads[5].wait()
         rows = q_ref[b]
         gate = nn(rows, fast[0])
         up = nn(rows, fast[1])
@@ -221,16 +259,24 @@
         out_ref[b, :, columns] = made[b, head]
 
     gradients(0)
-    pl.semaphore_wait(barrier, len(HOPS) + len(STEPS) + 1)
+    pl.semaphore_wait(barrier, len(STEPS) + 3)
+    ring_signal(0)
     start_pair(0)
     start_shares(0)
-    finish_shares(0)
+    ring_wait(0)
+    ring_signal(1)
+    start_wholes(0)
+    ring_wait(1)
+    ring_signal(2)
+    finish_wholes(0)
     update(0)
     gradients(1)
     start_pair(1)
     start_shares(1)
+    ring_wait(2)
     answer(0)
-    finish_shares(1)
+    start_wholes(1)
+    finish_wholes(1)
     update(1)
     answer(1)
     for b in range(BLOCKS):
@@ -249,13 +295,17 @@
     bf16, f32 = jnp.bfloat16, jnp.float32
     others, hops = len(STEPS), len(HOPS)
     vmem = pl.BlockSpec(memory_space=pltpu.VMEM)
+    hbm = pl.BlockSpec(memory_space=pltpu.HBM)
     dma = pltpu.SemaphoreType.DMA
     return pl.pallas_call(
         kernel,
         out_shape=jax.ShapeDtypeStruct((BLOCKS, OWN, HEADS * DH), bf16),
-        in_specs=[pl.BlockSpec(memory_space=pltpu.SMEM)] + [vmem] * 6,
+        in_specs=[pl.BlockSpec(memory_space=pltpu.SMEM)] + [hbm] * 6,
         out_specs=vmem,
         scratch_shapes=[
+            pltpu.VMEM((BLOCKS, DH, DH), bf16),
+            pltpu.VMEM((BLOCKS, DH, DH), bf16),
+            pltpu.VMEM((BLOCKS, DH, DH), bf16),
             pltpu.VMEM((BLOCKS, 2, 3, DH, HALF), bf16),
             pltpu.VMEM((BLOCKS, 3, DH, HALF), bf16),
             pltpu.VMEM((BLOCKS, CHIPS, 3, OWN, HALF), bf16),
@@ -263,8 +313,8 @@
             pltpu.VMEM((BLOCKS, 2, CHIPS, 3, OWN, HALF), bf16),
             pltpu.VMEM((3, DH, FH), f32),
             pltpu.VMEM((3, DH, FH), bf16),
-            pltpu.VMEM((3, DH, FH), f32),
             pltpu.VMEM((BLOCKS, HEADS, OWN, DH), bf16),
+            dma((6,)),
             dma((BLOCKS, 3)),
             dma((BLOCKS, 3)),
             dma((BLOCKS, others)),
@@ -275,9 +325,10 @@
             dma((BLOCKS, others + 1)),
             dma((BLOCKS, hops)),
             dma((BLOCKS, hops)),
+            pltpu.SemaphoreType.REGULAR((len(RING),)),
         ],
         compiler_params=pltpu.CompilerParams(
-            collective_id=0, has_side_effects=True, vmem_limit_bytes=48 * 1024 * 1024
+            collective_id=0, has_side_effects=True, vmem_limit_bytes=66_500_000
         ),
         name="ttt",
     )(learn_rates, queries, key_vectors, value_vectors, gate_weight, up_weight, down_weight)

time: 76.9 us -> 66.5 us (0.86)
  Pallas kernels: 69.6 us -> 64 us
  local copies, waits for them, and re-layouts: 6.4 us -> 1.67 us
    pallas_call x1, Pallas kernels: 69.6 us -> 64 us  [on_device(): pl.pallas_call(kernel, out_shape=jax.ShapeDtypeStruct((BLOCKS, OWN, HEADS...]
    unnamed x13 -> x1, local copies, waits for them, and re-layouts: 6.4 us -> 1.67 us
where the time goes in v2:
time: 66.5 us; the launch traced here: 66.4 us
  Pallas kernels  64 us (96%)
  local copies, waits for them, and re-layouts  1.67 us (3%)
    pallas_call x1, Pallas kernels, on_device(): pl.pallas_call(kernel, out_shape=jax.ShapeDtypeStruct((BLOCKS, OWN, HEADS...  64 us
    unnamed x1, local copies, waits for them, and re-layouts  1.67 us

profile of v2, /device:TPU:1, one launch (start us, length us, event | category | flops | bytes accessed | tf_op | source)
XLA Modules:
  0.0 66.4 jit_solution(16890428217427347435)
XLA Ops:
  0.7 64.0 %ttt.1 = bf16[2,16,4096]{2,1,0:T(8,128)(2,1)} custom-call(f32[1]{0:T(128)S(6)} %copy.9.lr_ref, bf16[2,256,256]{2,1,0:T(8,128)(2,1)} %q_hbm.1, bf16[2,256,256]{2,1,0:T(8,128)(2,1)} %k_hbm.1, bf16[2,256,256]{2,1,0:T(8,128)(2,1)} %v_hbm.1, bf16[1,256,512]{2,1,0:T(8,128)(2,1)} %wg_hbm.1, bf16[1,256,512]{2,1,0:T(8,128)(2,1)} %wu_hbm.1, bf16[1,256,512]{2,1,0:T(8,128)(2,1)} %wd_hbm.1), custom_call_target="tpu_custom_call" | custom-call | tf_op jit(solution)/shard_map/ttt/pallas_call | solution.py:300
  64.7 1.7 %copy.10 = bf16[2,16,4096]{2,1,0:T(8,128)(2,1)} copy(bf16[2,16,4096]{2,1,0:T(8,128)(2,1)} %ttt.1) | data formatting | bytes 524288

commit v3 on v2

v3 whole, which is shorter than its diff:
```python
import jax
import jax.numpy as jnp
from jax import lax
from jax.experimental import pallas as pl
from jax.experimental.pallas import tpu as pltpu
from jax.sharding import PartitionSpec as P

BLOCKS = 2
NS_ITERS = 3
COEF_A = 3.4445
COEF_B = -4.775
COEF_C = 2.0315
EPSILON = 1e-06

SIDE = 4
CHIPS = SIDE * SIDE
HEADS = 16
DH = 256
FH = 512
HALF = 256
OWN = DH // CHIPS
MESH = pl.DeviceIdType.MESH

STEPS = sorted(
    [(dx, dy) for dx in range(SIDE) for dy in range(SIDE) if (dx, dy) != (0, 0)],
    key=lambda s: -(min(s[0], SIDE - s[0]) + min(s[1], SIDE - s[1])),
)
RING = (1, 2, 4)
ORDER = (2, 1, 0)
PARTS = 2
HOPS = sorted(range(1, HEADS), key=lambda o: -min(o, HEADS - o))


def nn(a, b):
    return jnp.dot(a, b, preferred_element_type=jnp.float32)


def nt(a, b):
    return lax.dot_general(a, b, (((1,), (1,)), ((), ())), preferred_element_type=jnp.float32)


def kernel(
    lr_ref,
    q_hbm,
    k_hbm,
    v_hbm,
    wg_hbm,
    wu_hbm,
    wd_hbm,
    out_ref,
    q_ref,
    k_ref,
    v_ref,
    mine,
    theirs,
    pairs,
    shares,
    whole,
    master,
    fast,
    made,
    load_s,
    pair_s,
    pair_r,
    share_s,
    share_r,
    whole_s,
    whole_r,
    twin_s,
    twin_r,
    out_s,
    out_r,
    ring,
):
    bf16, f32 = jnp.bfloat16, jnp.float32
    head = lax.axis_index("head")
    ctx = lax.axis_index("ctx")
    core = ctx % 2
    chip = ctx // 2
    x, y = chip // SIDE, chip % SIDE
    twin = {"ctx": ctx + 1 - 2 * core}

    def to_chip(step, sign=1):
        return (x + sign * step[0] + SIDE) % SIDE * SIDE + (y + sign * step[1] + SIDE) % SIDE

    def on_chip(other):
        return {"ctx": other * 2 + core}

    def send(src, dst, s, r, device):
        return pltpu.make_async_remote_copy(
            src_ref=src,
            dst_ref=dst,
            send_sem=s,
            recv_sem=r,
            device_id=device,
            device_id_type=MESH,
        )

    def load(i, src, dst):
        return pltpu.make_async_copy(src, dst, load_s.at[i])

    first = [
        load(0, k_hbm.at[0], k_ref.at[0]),
        load(1, wg_hbm.at[0], fast.at[0]),
        load(2, wu_hbm.at[0], fast.at[1]),
        load(3, v_hbm.at[0], v_ref.at[0]),
        load(4, wd_hbm.at[0], fast.at[2]),
    ]
    second = [load(5, k_hbm.at[1], k_ref.at[1]), load(6, v_hbm.at[1], v_ref.at[1])]
    for copy in first:
        copy.start()

    barrier = pltpu.get_barrier_semaphore()
    for z in (1, HEADS - 1):
        pl.semaphore_signal(
            barrier, inc=1, device_id={"head": (head + z) % HEADS}, device_id_type=MESH
        )
    for step in STEPS:
        pl.semaphore_signal(
            barrier, inc=1, device_id=on_chip(to_chip(step)), device_id_type=MESH
        )
    pl.semaphore_signal(barrier, inc=1, device_id=twin, device_id_type=MESH)

    def ring_signal(level):
        for z in (RING[level], HEADS - RING[level]):
            pl.semaphore_signal(
                ring.at[level], inc=1, device_id={"head": (head + z) % HEADS}, device_id_type=MESH
            )

    def ring_wait(level):
        pl.semaphore_wait(ring.at[level], 2)

    def load_queries():
        for b in range(BLOCKS):
            for i, o in enumerate(HOPS + [0]):
                rows = pl.ds(pl.multiple_of((head + o) % HEADS * OWN, OWN), OWN)
                load(7, q_hbm.at[b, rows], q_ref.at[b, i]).start()

    def pair_copy(b, m):
        return send(
            mine.at[b, 1 - core, m], theirs.at[b, m], pair_s.at[b, m], pair_r.at[b, m], twin
        )

    def share_copy(b, m, i):
        other = to_chip(STEPS[i])
        return send(
            pairs.at[b, m, other],
            shares.at[b, m, i],
            share_s.at[b, m],
            share_r.at[b, m],
            on_chip(other),
        )

    def all_shares(b, m):
        block = shares.at[b, m]
        return send(block, block, share_s.at[b, m], share_r.at[b, m], twin)

    def whole_copy(b, m, i):
        here = whole.at[b, m, core, chip]
        return send(
            here, here, whole_s.at[b, m], whole_r.at[b, m, i], on_chip(to_chip(STEPS[i]))
        )

    def all_wholes(b, m):
        block = shares.at[b, m]
        return send(block, block, whole_s.at[b, m], whole_r.at[b, m, 0], twin)

    def twin_copy(b, m, slot):
        here = whole.at[b, m, core, slot]
        return send(here, here, twin_s.at[b, m], twin_r.at[b, m], twin)

    def all_twins(b, m):
        block = whole.at[b, m, 1 - core]
        return send(block, block, twin_s.at[b, m], twin_r.at[b, m], twin)

    columns = pl.ds(pl.multiple_of(head * DH, DH), DH)

    def out_copy(b, i):
        return send(
            made.at[b, i],
            out_ref.at[b, :, columns],
            out_s.at[b],
            out_r.at[b],
            {"head": (head + HOPS[i]) % HEADS},
        )

    def all_outs(b):
        block = made.at[b, pl.ds(0, len(HOPS))]
        return send(block, block, out_s.at[b], out_r.at[b], twin)

    def gradients(b):
        def hand_over(m, rows_t, d):
            for j in range(2):
                mine[b, j, m] = nn(rows_t, d[:, j * HALF : (j + 1) * HALF]).astype(bf16)

        if b == 0:
            for copy in first[:3]:
                copy.wait()
        else:
            for copy in second:
                copy.wait()
        keys = k_ref[b]
        gate = nn(keys, fast[0])
        up = nn(keys, fast[1])
        sig = jax.nn.sigmoid(gate)
        act = gate * sig
        gated = (act * up).astype(bf16)
        if b == 0:
            for copy in first[3:]:
                copy.wait()
        values = v_ref[b]
        hand_over(2, values.T, gated)
        if b == 0:
            pl.semaphore_wait(barrier, len(STEPS) + 3)
            ring_signal(0)
        pair_copy(b, 2).start()
        back = nn(values, fast[2])
        keys_t = keys.T
        hand_over(1, keys_t, (back * act).astype(bf16))
        pair_copy(b, 1).start()
        d_gate = (back * up * sig * (1.0 + gate * (1.0 - sig))).astype(bf16)
        hand_over(0, keys_t, d_gate)
        pair_copy(b, 0).start()

    def start_shares(b):
        for m in ORDER:
            pair_copy(b, m).wait_recv()
            both = mine[b, core, m].astype(f32) + theirs[b, m].astype(f32)
            pairs[b, m] = both.astype(bf16).reshape(CHIPS, OWN, HALF)
            for i in range(len(STEPS)):
                share_copy(b, m, i).start()

    def start_wholes(b):
        for m in ORDER:
            all_shares(b, m).wait_recv()
            total = pairs[b, m, chip].astype(f32)
            for i in range(len(STEPS)):
                total = total + shares[b, m, i].astype(f32)
            whole[b, m, core, chip] = total.astype(bf16)
            for i in range(len(STEPS)):
                whole_copy(b, m, i).start()
            twin_copy(b, m, chip).start()

    def forward(b, m):
        for i in range(len(STEPS)):
            whole_copy(b, m, i).wait_recv()
            twin_copy(b, m, to_chip(STEPS[i], -1)).start()

    def finish_wholes(b):
        forward(b, 2)
        forward(b, 1)
        all_twins(b, 2).wait_recv()
        update(b, (2,))
        forward(b, 0)
        all_twins(b, 1).wait_recv()
        all_twins(b, 0).wait_recv()
        update(b, (0, 1))

    def update(b, which):
        now_b = [
            jnp.concatenate([whole[b, m, j].reshape(DH, HALF) for j in range(2)], axis=1)
            for m in which
        ]
        now = [g.astype(f32) for g in now_b]
        sizes = [jnp.sum(g * g, keepdims=True) for g in now]
        scales = [1.0 / (jnp.sqrt(size) + EPSILON) for size in sizes]
        for turn in range(NS_ITERS):
            grams = [nt(g, g) for g in now_b]
            if turn == 0:
                grams = [g * s * s for g, s in zip(grams, scales)]
            grams_b = [g.astype(bf16) for g in grams]
            polys = [COEF_B * g + COEF_C * nn(h, h) for g, h in zip(grams, grams_b)]
            now = [
                COEF_A * g + nn(poly.astype(bf16), h) for g, poly, h in zip(now, polys, now_b)
            ]
            if turn == 0:
                now = [g * s for g, s in zip(now, scales)]
            now_b = [g.astype(bf16) for g in now]
        for m, step in zip(which, now):
            before = fast[m].astype(f32) if b == 0 else master[m]
            moved = before + lr_ref[0] * step
            if b + 1 < BLOCKS:
                master[m] = moved
            fast[m] = moved.astype(bf16)

    def answer(b):
        for part in range(PARTS):
            size = HEADS // PARTS
            rows = q_ref[b, part * size : (part + 1) * size].reshape(size * OWN, DH)
            gate = nn(rows, fast[0])
            up = nn(rows, fast[1])
            gated = (gate * jax.nn.sigmoid(gate) * up).astype(bf16)
            results = nt(gated, fast[2]).astype(bf16)
            made[b, part * size : (part + 1) * size] = results.reshape(size, OWN, DH)
            for i in range(part * size, min((part + 1) * size, len(HOPS))):
                out_copy(b, i).start()
        out_ref[b, :, columns] = made[b, len(HOPS)]

    gradients(0)
    start_shares(0)
    for copy in second:
        copy.start()
    load_queries()
    ring_wait(0)
    ring_signal(1)
    start_wholes(0)
    ring_wait(1)
    ring_signal(2)
    finish_wholes(0)
    gradients(1)
    start_shares(1)
    ring_wait(2)
    load(7, q_ref, q_ref).wait()
    answer(0)
    start_wholes(1)
    finish_wholes(1)
    answer(1)
    for b in range(BLOCKS):
        for m in ORDER:
            pair_copy(b, m).wait_send()
            all_shares(b, m).wait_send()
            all_wholes(b, m).wait_send()
            all_twins(b, m).wait_send()
        all_outs(b).wait()


def on_device(*operands):
    *arrays, learn_rates = operands
    bf16, f32 = jnp.bfloat16, jnp.float32
    others = len(STEPS)
    vmem = pl.BlockSpec(memory_space=pltpu.VMEM)
    hbm = pl.BlockSpec(memory_space=pltpu.HBM)
    dma = pltpu.SemaphoreType.DMA
    return pl.pallas_call(
        kernel,
        out_shape=jax.ShapeDtypeStruct((BLOCKS, OWN, HEADS * DH), bf16),
        in_specs=[pl.BlockSpec(memory_space=pltpu.SMEM)] + [hbm] * 6,
        out_specs=vmem,
        scratch_shapes=[
            pltpu.VMEM((BLOCKS, HEADS, OWN, DH), bf16),
            pltpu.VMEM((BLOCKS, DH, DH), bf16),
            pltpu.VMEM((BLOCKS, DH, DH), bf16),
            pltpu.VMEM((BLOCKS, 2, 3, DH, HALF), bf16),
            pltpu.VMEM((BLOCKS, 3, DH, HALF), bf16),
            pltpu.VMEM((BLOCKS, 3, CHIPS, OWN, HALF), bf16),
            pltpu.VMEM((BLOCKS, 3, others, OWN, HALF), bf16),
            pltpu.VMEM((BLOCKS, 3, 2, CHIPS, OWN, HALF), bf16),
            pltpu.VMEM((3, DH, FH), f32),
            pltpu.VMEM((3, DH, FH), bf16),
            pltpu.VMEM((BLOCKS, HEADS, OWN, DH), bf16),
            dma((8,)),
            dma((BLOCKS, 3)),
            dma((BLOCKS, 3)),
            dma((BLOCKS, 3)),
            dma((BLOCKS, 3)),
            dma((BLOCKS, 3)),
            dma((BLOCKS, 3, others)),
            dma((BLOCKS, 3)),
            dma((BLOCKS, 3)),
            dma((BLOCKS,)),
            dma((BLOCKS,)),
            pltpu.SemaphoreType.REGULAR((len(RING),)),
        ],
        compiler_params=pltpu.CompilerParams(
            collective_id=0, has_side_effects=True, vmem_limit_bytes=50_000_000
        ),
        name="ttt",
    )(learn_rates, *[pltpu.with_memory_space_constraint(array, pltpu.HBM) for array in arrays])


def solution(mesh):
    return jax.shard_map(
        on_device,
        mesh=mesh,
        in_specs=(
            P(None, "ctx", "head"),
            P(None, "ctx", "head"),
            P(None, "ctx", "head"),
            P("head", None, None),
            P("head", None, None),
            P("head", None, None),
            P("head"),
        ),
        out_specs=P(None, ("ctx", "head"), None),
        check_vma=False,
    )
```

time: 66.5 us -> 62.1 us (0.934)
  Pallas kernels: 64 us -> 60.6 us
  local copies, waits for them, and re-layouts: 1.67 us -> 0.71 us
    pallas_call x1, Pallas kernels: 64 us -> 60.6 us  [on_device(): pl.pallas_call(kernel, out_shape=jax.ShapeDtypeStruct((BLOCKS, OWN, HEADS...]
    unnamed x1, local copies, waits for them, and re-layouts: 1.67 us -> 0.71 us
where the time goes in v3:
time: 62.1 us; the launch traced here: 62 us
  Pallas kernels  60.6 us (98%)
  local copies, waits for them, and re-layouts  0.71 us (1%)
  between operations  0.66 us (1%)
    pallas_call x1, Pallas kernels, on_device(): pl.pallas_call(kernel, out_shape=jax.ShapeDtypeStruct((BLOCKS, OWN, HEADS...  60.6 us

profile of v3, /device:TPU:1, one launch (start us, length us, event | category | flops | bytes accessed | tf_op | source)
XLA Modules:
  0.0 62.0 jit_solution(4948501723355915407)
XLA Ops:
  0.7 60.6 %ttt.1 = bf16[2,16,4096]{2,1,0:T(8,128)(2,1)S(1)} custom-call(f32[1]{0:T(128)S(6)} %copy.9.lr_ref, bf16[2,256,256]{2,1,0:T(8,128)(2,1)} %q_hbm.1, bf16[2,256,256]{2,1,0:T(8,128)(2,1)} %k_hbm.1, bf16[2,256,256]{2,1,0:T(8,128)(2,1)} %v_hbm.1, bf16[1,256,512]{2,1,0:T(8,128)(2,1)} %wg_hbm.1, bf16[1,256,512]{2,1,0:T(8,128)(2,1)} %wu_hbm.1, ...), custom_call_target="tpu_custom_call" | custom-call | tf_op jit(solution)/shard_map/ttt/pallas_call | solution.py:334
  61.3 0.7 %copy.10 = bf16[2,16,4096]{2,1,0:T(8,128)(2,1)} copy(bf16[2,16,4096]{2,1,0:T(8,128)(2,1)S(1)} %ttt.1) | data formatting | bytes 524288

commit v4 on v3

--- a/solution.py
+++ b/solution.py
@@ -237,12 +237,12 @@
             for i in range(len(STEPS)):
                 total = total + shares[b, m, i].astype(f32)
             whole[b, m, core, chip] = total.astype(bf16)
+            twin_copy(b, m, chip).start()
             for i in range(len(STEPS)):
                 whole_copy(b, m, i).start()
-            twin_copy(b, m, chip).start()
 
     def forward(b, m):
-        for i in range(len(STEPS)):
+        for i in reversed(range(len(STEPS))):
             whole_copy(b, m, i).wait_recv()
             twin_copy(b, m, to_chip(STEPS[i], -1)).start()
 
@@ -250,13 +250,12 @@
         forward(b, 2)
         forward(b, 1)
         all_twins(b, 2).wait_recv()
-        update(b, (2,))
-        forward(b, 0)
+        update(b, (2,), lambda: forward(b, 0))
         all_twins(b, 1).wait_recv()
         all_twins(b, 0).wait_recv()
         update(b, (0, 1))
 
-    def update(b, which):
+    def update(b, which, between=None):
         now_b = [
             jnp.concatenate([whole[b, m, j].reshape(DH, HALF) for j in range(2)], axis=1)
             for m in which
@@ -273,6 +272,8 @@
             now = [
                 COEF_A * g + nn(poly.astype(bf16), h) for g, poly, h in zip(now, polys, now_b)
             ]
+            if turn == 1 and between is not None:
+                between()
             if turn == 0:
                 now = [g * s for g, s in zip(now, scales)]
             now_b = [g.astype(bf16) for g in now]

time: 62.1 us -> 61.6 us (level)
  no operation moved by 1% of the time
where the time goes in v4:
time: 61.6 us; the launch traced here: 61.5 us
  Pallas kernels  60.1 us (98%)
  local copies, waits for them, and re-layouts  0.71 us (1%)
  between operations  0.66 us (1%)
    pallas_call x1, Pallas kernels, on_device(): pl.pallas_call(kernel, out_shape=jax.ShapeDtypeStruct((BLOCKS, OWN, HEADS...  60.1 us

profile of v4, /device:TPU:1, one launch (start us, length us, event | category | flops | bytes accessed | tf_op | source)
XLA Modules:
  0.0 61.5 jit_solution(10608075267624460922)
XLA Ops:
  0.7 60.1 %ttt.1 = bf16[2,16,4096]{2,1,0:T(8,128)(2,1)S(1)} custom-call(f32[1]{0:T(128)S(6)} %copy.9.lr_ref, bf16[2,256,256]{2,1,0:T(8,128)(2,1)} %q_hbm.1, bf16[2,256,256]{2,1,0:T(8,128)(2,1)} %k_hbm.1, bf16[2,256,256]{2,1,0:T(8,128)(2,1)} %v_hbm.1, bf16[1,256,512]{2,1,0:T(8,128)(2,1)} %wg_hbm.1, bf16[1,256,512]{2,1,0:T(8,128)(2,1)} %wu_hbm.1, ...), custom_call_target="tpu_custom_call" | custom-call | tf_op jit(solution)/shard_map/ttt/pallas_call | solution.py:335
  60.8 0.7 %copy.10 = bf16[2,16,4096]{2,1,0:T(8,128)(2,1)} copy(bf16[2,16,4096]{2,1,0:T(8,128)(2,1)S(1)} %ttt.1) | data formatting | bytes 524288

commit v5 on v4

--- a/solution.py
+++ b/solution.py
@@ -59,6 +59,8 @@
     master,
     fast,
     made,
+    turned,
+    back_ref,
     load_s,
     pair_s,
     pair_r,
@@ -196,9 +198,6 @@
         if b == 0:
             for copy in first[:3]:
                 copy.wait()
-        else:
-            for copy in second:
-                copy.wait()
         keys = k_ref[b]
         gate = nn(keys, fast[0])
         up = nn(keys, fast[1])
@@ -209,13 +208,13 @@
             for copy in first[3:]:
                 copy.wait()
         values = v_ref[b]
-        hand_over(2, values.T, gated)
+        hand_over(2, values.T if b == 0 else turned[1], gated)
         if b == 0:
             pl.semaphore_wait(barrier, len(STEPS) + 3)
             ring_signal(0)
         pair_copy(b, 2).start()
-        back = nn(values, fast[2])
-        keys_t = keys.T
+        back = nn(values, fast[2]) if b == 0 else back_ref[...]
+        keys_t = keys.T if b == 0 else turned[0]
         hand_over(1, keys_t, (back * act).astype(bf16))
         pair_copy(b, 1).start()
         d_gate = (back * up * sig * (1.0 + gate * (1.0 - sig))).astype(bf16)
@@ -251,6 +250,8 @@
         forward(b, 1)
         all_twins(b, 2).wait_recv()
         update(b, (2,), lambda: forward(b, 0))
+        if b + 1 < BLOCKS:
+            back_ref[...] = nn(v_ref[b + 1], fast[2])
         all_twins(b, 1).wait_recv()
         all_twins(b, 0).wait_recv()
         update(b, (0, 1))
@@ -307,6 +308,10 @@
     start_wholes(0)
     ring_wait(1)
     ring_signal(2)
+    for copy in second:
+        copy.wait()
+    turned[0] = k_ref[1].T
+    turned[1] = v_ref[1].T
     finish_wholes(0)
     gradients(1)
     start_shares(1)
@@ -349,6 +354,8 @@
             pltpu.VMEM((3, DH, FH), f32),
             pltpu.VMEM((3, DH, FH), bf16),
             pltpu.VMEM((BLOCKS, HEADS, OWN, DH), bf16),
+            pltpu.VMEM((2, DH, DH), bf16),
+            pltpu.VMEM((DH, FH), f32),
             dma((8,)),
             dma((BLOCKS, 3)),
             dma((BLOCKS, 3)),

time: 61.6 us -> 62.7 us (1.018)
  Pallas kernels: 60.1 us -> 61.2 us
    pallas_call x1, Pallas kernels: 60.1 us -> 61.2 us  [on_device(): pl.pallas_call(kernel, out_shape=jax.ShapeDtypeStruct((BLOCKS, OWN, HEADS...]
where the time goes in v5:
time: 62.7 us; the launch traced here: 62.5 us
  Pallas kernels  61.2 us (98%)
  local copies, waits for them, and re-layouts  0.71 us (1%)
  between operations  0.66 us (1%)
    pallas_call x1, Pallas kernels, on_device(): pl.pallas_call(kernel, out_shape=jax.ShapeDtypeStruct((BLOCKS, OWN, HEADS...  61.2 us

profile of v5, /device:TPU:1, one launch (start us, length us, event | category | flops | bytes accessed | tf_op | source)
XLA Modules:
  0.0 62.5 jit_solution(13373980501461929495)
XLA Ops:
  0.7 61.2 %ttt.1 = bf16[2,16,4096]{2,1,0:T(8,128)(2,1)S(1)} custom-call(f32[1]{0:T(128)S(6)} %copy.9.lr_ref, bf16[2,256,256]{2,1,0:T(8,128)(2,1)} %q_hbm.1, bf16[2,256,256]{2,1,0:T(8,128)(2,1)} %k_hbm.1, bf16[2,256,256]{2,1,0:T(8,128)(2,1)} %v_hbm.1, bf16[1,256,512]{2,1,0:T(8,128)(2,1)} %wg_hbm.1, bf16[1,256,512]{2,1,0:T(8,128)(2,1)} %wu_hbm.1, ...), custom_call_target="tpu_custom_call" | custom-call | tf_op jit(solution)/shard_map/ttt/pallas_call | solution.py:340
  61.8 0.7 %copy.10 = bf16[2,16,4096]{2,1,0:T(8,128)(2,1)} copy(bf16[2,16,4096]{2,1,0:T(8,128)(2,1)S(1)} %ttt.1) | data formatting | bytes 524288
